TPU v7x, 32 devices: a whole 2x2x4 slice. The times are simulated.
32 devices in a mesh: row: 4 (over z), col: 2 (over y), depth: 4 (over x, core).
Axes of the slice: x: 2, y: 2, z: 4, core: 2. Of those that a mesh axis runs over, the one named last changes fastest.
Arguments:
- right_sides: float32 [64, 4096], P('depth', ('row', 'col')), may hold values from -12 to 12
- blocks: float32 [4, 2, 16, 256, 256], P('row', 'col'), may hold values from -0.06 to 6.1, as said below
- block_rows: int32 [4, 2, 16], P('row', 'col'), may hold values from 0 to 3, as said below
- block_cols: int32 [4, 2, 16], P('row', 'col'), may hold values from 0 to 7, as said below
- block_count: int32 [4, 2], P('row', 'col'), may hold values from 2 to 16
Outputs:
- solution: float32 [64, 4096], P('depth', ('row', 'col'))
- residual: float32 [64, 4096], P('depth', ('row', 'col'))
Inputs may be any that keep to these rules, and one draw needn't show every extreme that they name: Slot s < 2 of row index r and col index c holds the diagonal block with block_rows = c * 2 + s and block_cols = r * 2 + s. The valid later slots name distinct blocks whose I is below J. At slots from block_count on, block_rows and block_cols hold 0; blocks there hold arbitrary values and are not part of A. `block_cols`: see block_rows. Diagonal-slot blocks are symmetric; A is positive definite. Slots from block_count on are not part of A.
All inputs are finite; a program needn't handle non-finite values.
Results may differ from a plain program's by a relative error of at most 0.0003.
Values sent between devices are 32-bit elements; how exact they have to be, the bound alone decides.
No kernel may reach another device: no remote copies, remote signals or barrier semaphores. Data moves between devices by JAX's collectives and lax.ppermute only.
A program may use at most 64 MiB of HBM per device.

v0:
```python
import jax
import jax.numpy as jnp
from jax import lax
from jax.sharding import PartitionSpec as P

BLK = 256
ITERS = 2
SEG = 2


def per_device(right_sides, blocks, block_rows, block_cols, block_count):
    highest = lax.Precision.HIGHEST
    own_width = right_sides.shape[0]
    depth_index = lax.axis_index("depth")
    tile_blocks = blocks[0, 0]
    rows_here = block_rows[0, 0]
    cols_here = block_cols[0, 0]
    live_count = block_count[0, 0]
    row_span = SEG * lax.axis_size("col")
    col_span = SEG * lax.axis_size("row")
    slot_index = jnp.arange(tile_blocks.shape[0], dtype=jnp.int32)
    residual_all = lax.all_gather(right_sides, "depth", axis=0, tiled=True)
    direction_all = residual_all
    solution = jnp.zeros_like(right_sides)
    current = lax.psum(jnp.dot(residual_all, residual_all.T, precision=highest), ("row", "col"))
    for iteration in range(ITERS):
        own_direction = lax.dynamic_slice_in_dim(
            direction_all, depth_index * own_width, own_width, 0
        )
        row_part = lax.all_gather(own_direction, "col", axis=1, tiled=True).reshape(
            own_width, row_span, BLK
        )
        col_part = lax.all_gather(own_direction, "row", axis=1, tiled=True).reshape(
            own_width, col_span, BLK
        )
        live_mask = (slot_index < live_count).astype(jnp.float32)
        mirror_mask = live_mask * (slot_index >= SEG).astype(jnp.float32)
        toward_rows = jnp.einsum(
            "csk,smk->csm", col_part[:, cols_here], tile_blocks, precision=highest
        )
        toward_cols = jnp.einsum(
            "csm,smk->csk", row_part[:, rows_here], tile_blocks, precision=highest
        )
        toward_rows = toward_rows * live_mask[None, :, None]
        toward_cols = toward_cols * mirror_mask[None, :, None]
        row_select = (rows_here[:, None] == jnp.arange(row_span, dtype=jnp.int32)[None, :]).astype(
            jnp.float32
        )
        col_select = (cols_here[:, None] == jnp.arange(col_span, dtype=jnp.int32)[None, :]).astype(
            jnp.float32
        )
        row_terms = jnp.einsum("si,csm->cim", row_select, toward_rows, precision=highest)
        col_terms = jnp.einsum("sj,csk->cjk", col_select, toward_cols, precision=highest)
        row_sum = lax.psum_scatter(
            row_terms.reshape(own_width, row_span * BLK), "col", scatter_dimension=1, tiled=True
        )
        col_sum = lax.psum_scatter(
            col_terms.reshape(own_width, col_span * BLK), "row", scatter_dimension=1, tiled=True
        )
        mapped = row_sum + col_sum
        mapped_all = lax.all_gather(mapped, "depth", axis=0, tiled=True)
        curvature, cross_gram, image_gram = lax.psum(
            (
                jnp.dot(direction_all, mapped_all.T, precision=highest),
                jnp.dot(residual_all, mapped_all.T, precision=highest),
                jnp.dot(mapped_all, mapped_all.T, precision=highest),
            ),
            ("row", "col"),
        )
        step_size = jax.scipy.linalg.cho_solve((jnp.linalg.cholesky(curvature), True), current)
        own_step = lax.dynamic_slice_in_dim(step_size, depth_index * own_width, own_width, 1)
        solution = solution + lax.dot_general(
            own_step, direction_all, (((0,), (0,)), ((), ())), precision=highest
        )
        residual_all = residual_all - lax.dot_general(
            step_size, mapped_all, (((0,), (0,)), ((), ())), precision=highest
        )
        if iteration + 1 < ITERS:
            coupling = jnp.dot(cross_gram, step_size, precision=highest)
            quadratic = lax.dot_general(
                step_size,
                jnp.dot(image_gram, step_size, precision=highest),
                (((0,), (0,)), ((), ())),
                precision=highest,
            )
            renewed = current - coupling - coupling.T + quadratic
            conjugate = jax.scipy.linalg.cho_solve((jnp.linalg.cholesky(current), True), renewed)
            direction_all = residual_all + lax.dot_general(
                conjugate, direction_all, (((0,), (0,)), ((), ())), precision=highest
            )
            current = renewed
    own_residual = lax.dynamic_slice_in_dim(residual_all, depth_index * own_width, own_width, 0)
    return (solution, own_residual)


def solution(mesh):
    return jax.shard_map(
        per_device,
        mesh=mesh,
        in_specs=(
            P("depth", ("row", "col")),
            P("row", "col", None, None, None),
            P("row", "col", None),
            P("row", "col", None),
            P("row", "col"),
        ),
        out_specs=(P("depth", ("row", "col")), P("depth", ("row", "col"))),
        check_vma=False,
    )
```

profile of v0, /device:TPU:0, one launch (start us, length us, event | category | flops | bytes accessed | tf_op | source)
XLA Modules:
  0.0 254.3 jit_solution(11665464484053111125)
XLA Ops:
  7.2 6.7 %all_gather.21 = f32[64,512]{1,0:T(8,128)S(1)} all-gather(f32[16,512]{1,0:T(8,128)} %param.8), channel_id=1, replica_groups=mesh['row'=4,'col'=2,'depth'=4] {'depth'}, dimensions={0}, use_global_device_ids=true | all-gather | bytes 163840 | tf_op jit(solution)/shard_map/all_gather | solution.py:22
  13.9 13.9 %all_gather.22 = f32[16,2048]{1,0:T(8,128)S(1)} all-gather(f32[16,512]{1,0:T(8,128)S(1)} %constant_dynamic-slice_fusion.1), channel_id=1, replica_groups=mesh['row'=4,'col'=2,'depth'=4] {'row'}, dimensions={1}, use_global_device_ids=true | all-gather | bytes 163840 | tf_op jit(solution)/shard_map/all_gather | solution.py:33
  27.9 0.7 fusion.57
  29.2 0.6 gather_fusion
  29.8 5.7 %fusion.6 = f32[16,16,256]{2,1,0:T(8,128)S(1)} fusion(f32[1,1,16,256,256]{4,3,2,1,0:T(8,128)} %param.9, f32[16,16,256]{2,1,0:T(8,128)S(1)} %gather_fusion), kind=kOutput, calls=%fused_computation.10 | convolution fusion | flops 201326592 | bytes 4718592 | tf_op jit(solution)/shard_map/csk,smk->csm/dot_general | solution.py:38
  35.5 0.4 fusion.17
  35.9 0.6 copy.36
  36.6 4.6 %all_gather.23 = f32[16,1024]{1,0:T(8,128)S(1)} all-gather(f32[16,512]{1,0:T(8,128)S(1)} %constant_dynamic-slice_fusion.1), channel_id=1, replica_groups=mesh['row'=4,'col'=2,'depth'=4] {'col'}, dimensions={1}, use_global_device_ids=true | all-gather | bytes 98304 | tf_op jit(solution)/shard_map/all_gather | solution.py:30
  41.2 0.6 gather_fusion.1
  41.8 4.3 %fusion.4 = f32[16,16,256]{2,1,0:T(8,128)S(1)} fusion(f32[1,1,16,256,256]{4,3,2,1,0:T(8,128)} %param.9, f32[16,16,256]{2,1,0:T(8,128)S(1)} %gather_fusion.1), kind=kOutput, calls=%fused_computation.8 | convolution fusion | flops 201326592 | bytes 4718592 | tf_op jit(solution)/shard_map/csm,smk->csk/dot_general | solution.py:41
  46.1 0.4 fusion.14
  46.5 0.7 copy.37
  47.2 0.3 fusion.59
  47.5 0.3 reduce-scatter.5.cloned.1.call-done
  47.8 21.8 %reduce-scatter.7.cloned.1.call-done = f32[16,512]{1,0:T(8,128)} async-done(((f32[16,2048]{1,0:T(8,128)}), f32[16,512]{1,0:T(8,128)}) %reduce-scatter.7.cloned.1.call-update) | async-done | bytes 32784 | tf_op jit(solution)/shard_map/reduce_scatter | solution.py:57
  69.6 0.8 add.75
  70.4 5.4 %all_gather.24 = f32[64,512]{1,0:T(8,128)S(1)} all-gather(f32[16,512]{1,0:T(8,128)S(1)} %add.75), channel_id=1, replica_groups=mesh['row'=4,'col'=2,'depth'=4] {'depth'}, dimensions={0}, use_global_device_ids=true | all-gather | bytes 163840 | tf_op jit(solution)/shard_map/all_gather | solution.py:61
  75.8 0.3 convolution_bitcast_fusion
  76.0 0.3 fusion.61
  76.3 35.3 %all-reduce = (f32[64,64]{0,1:T(8,128)S(1)}, f32[64,64]{0,1:T(8,128)S(1)}, f32[64,64]{1,0:T(8,128)S(1)}) all-reduce(f32[64,64]{0,1:T(8,128)S(1)} %fusion.59, f32[64,64]{0,1:T(8,128)S(1)} %convolution_bitcast_fusion, f32[64,64]{1,0:T(8,128)S(1)} %fusion.61), channel_id=1, replica_groups=mesh['row'=4,'col'=2,'depth'=4] {'row','col'}, use_global_device_ids=true, to_apply=%region_5.7 | all-reduce | flops 12288 | bytes 98304 | tf_op jit(solution)/shard_map/psum | solution.py:25
  111.7 0.1 copy.16
  111.8 5.8 %cholesky.59 = f32[64,64]{1,0:T(8,128)S(1)} custom-call(f32[64,64]{1,0:T(8,128)S(1)} %get-tuple-element.8), custom_call_target="Cholesky" | custom-call | tf_op jit(solution)/shard_map/jit(cholesky)/cholesky | solution.py:70
  117.7 0.6 compare_reduce_fusion.2
  118.3 0.7 fusion.24
  119.0 4.9 %custom-call.9 = f32[1,64,64]{1,2,0:T(8,128)S(1)} custom-call(f32[1,64,64]{2,1,0:T(8,128)S(1)} %fusion.24), custom_call_target="InvertDiagBlocksLowerTriangular" | custom-call | tf_op jit(solution)/shard_map/jit(_cho_solve)/triangular_solve | solution.py:70
  123.9 0.2 fusion.39
  124.2 0.2 fusion.37
  124.4 0.3 convolution_subtract_fusion
  124.7 0.2 fusion.60
  124.9 0.2 fusion.62
  125.2 5.9 %cholesky.70 = f32[64,64]{1,0:T(8,128)S(1)} custom-call(f32[64,64]{1,0:T(8,128)S(1)} %get-tuple-element.7), custom_call_target="Cholesky" | custom-call | tf_op jit(solution)/shard_map/jit(cholesky)/cholesky | solution.py:87
  131.1 0.6 compare_reduce_fusion.1
  131.7 0.7 fusion.25
  132.4 4.9 %custom-call.10 = f32[1,64,64]{1,2,0:T(8,128)S(1)} custom-call(f32[1,64,64]{2,1,0:T(8,128)S(1)} %fusion.25), custom_call_target="InvertDiagBlocksLowerTriangular" | custom-call | tf_op jit(solution)/shard_map/jit(_cho_solve)/triangular_solve | solution.py:87
  137.3 0.3 convolution_add_fusion.2
  137.5 0.2 fusion.34
  137.8 0.2 fusion.32
  137.9 0.3 convolution_add_fusion
  138.3 13.3 %all_gather.25 = f32[16,2048]{1,0:T(8,128)S(1)} all-gather(f32[16,512]{1,0:T(8,128)S(1)} %constant_dynamic-slice_fusion), channel_id=1, replica_groups=mesh['row'=4,'col'=2,'depth'=4] {'row'}, dimensions={1}, use_global_device_ids=true | all-gather | bytes 163840 | tf_op jit(solution)/shard_map/all_gather | solution.py:33
  151.6 4.6 %all_gather.26 = f32[16,1024]{1,0:T(8,128)S(1)} all-gather(f32[16,512]{1,0:T(8,128)S(1)} %constant_dynamic-slice_fusion), channel_id=1, replica_groups=mesh['row'=4,'col'=2,'depth'=4] {'col'}, dimensions={1}, use_global_device_ids=true | all-gather | bytes 98304 | tf_op jit(solution)/shard_map/all_gather | solution.py:30
  156.2 0.6 gather_fusion.2
  156.8 5.7 %fusion.2 = f32[16,16,256]{2,1,0:T(8,128)S(1)} fusion(f32[1,1,16,256,256]{4,3,2,1,0:T(8,128)} %param.9, f32[16,16,256]{2,1,0:T(8,128)S(1)} %gather_fusion.2), kind=kOutput, calls=%fused_computation.6 | convolution fusion | flops 201326592 | bytes 4718592 | tf_op jit(solution)/shard_map/csk,smk->csm/dot_general | solution.py:38
  162.5 0.4 fusion.11
  162.9 0.6 copy.38
  163.6 0.6 gather_fusion.3
  164.2 4.3 %fusion = f32[16,16,256]{2,1,0:T(8,128)S(1)} fusion(f32[1,1,16,256,256]{4,3,2,1,0:T(8,128)} %param.9, f32[16,16,256]{2,1,0:T(8,128)S(1)} %gather_fusion.3), kind=kOutput, calls=%fused_computation.4 | convolution fusion | flops 201326592 | bytes 4718592 | tf_op jit(solution)/shard_map/csm,smk->csk/dot_general | solution.py:41
  168.5 0.4 fusion.8
  168.8 0.7 copy.39
  169.5 0.2 fusion.43
  169.7 1.3 reduce-scatter.9.cloned.1.call-done
  171.0 21.6 %reduce-scatter.11.cloned.1.call-done = f32[16,512]{1,0:T(8,128)} async-done(((f32[16,2048]{1,0:T(8,128)}), f32[16,512]{1,0:T(8,128)}) %reduce-scatter.11.cloned.1.call-update) | async-done | bytes 32784 | tf_op jit(solution)/shard_map/reduce_scatter | solution.py:57
  192.6 0.8 add.78
  193.4 5.4 %all_gather.27 = f32[64,512]{1,0:T(8,128)S(1)} all-gather(f32[16,512]{1,0:T(8,128)S(1)} %add.78), channel_id=1, replica_groups=mesh['row'=4,'col'=2,'depth'=4] {'depth'}, dimensions={0}, use_global_device_ids=true | all-gather | bytes 163840 | tf_op jit(solution)/shard_map/all_gather | solution.py:61
  198.8 0.3 fusion.63
  199.1 34.3 %psum.34 = f32[64,64]{0,1:T(8,128)S(1)} all-reduce(f32[64,64]{0,1:T(8,128)S(1)} %fusion.63), channel_id=1, replica_groups=mesh['row'=4,'col'=2,'depth'=4] {'row','col'}, use_global_device_ids=true, to_apply=%region_9.12 | all-reduce | flops 4096 | bytes 32768 | tf_op jit(solution)/shard_map/psum | solution.py:62
  233.5 5.8 %cholesky.81 = f32[64,64]{1,0:T(8,128)S(1)} custom-call(f32[64,64]{1,0:T(8,128)S(1)} %fusion.31), custom_call_target="Cholesky" | custom-call | tf_op jit(solution)/shard_map/jit(cholesky)/cholesky | solution.py:70
  239.4 0.6 compare_reduce_fusion
  240.0 0.7 fusion.26
  240.7 4.9 %custom-call.11 = f32[1,64,64]{1,2,0:T(8,128)S(1)} custom-call(f32[1,64,64]{2,1,0:T(8,128)S(1)} %fusion.26), custom_call_target="InvertDiagBlocksLowerTriangular" | custom-call | tf_op jit(solution)/shard_map/jit(_cho_solve)/triangular_solve | solution.py:70
  245.6 0.2 fusion.29
  245.8 0.2 fusion.27
  246.1 0.3 fusion.64
  246.3 0.8 convolution_add_fusion.1
  247.2 0.6 dynamic-slice_subtract_fusion
  (31 shorter events, 0.7 us)
Async XLA Ops:
  7.2 28.4 %copy-start = (s32[1,1,16]{2,1,0:T(1,128)S(1)}, s32[1,1,16]{2,1,0:T(1,128)}, u32[]{:S(2)}) copy-start(s32[1,1,16]{2,1,0:T(1,128)} %param.10) | copy-start | bytes 196
  7.2 40.7 %reduce-scatter.5.cloned.1.call-start = ((), (), s32[]{:S(2)}) async-start(), calls=%async_computation.4 | async-start | bytes 98304 | tf_op jit(solution)/shard_map/reduce_scatter | solution.py:54
  29.8 16.3 %copy-start.1 = (s32[1,1,16]{2,1,0:T(1,128)S(1)}, s32[1,1,16]{2,1,0:T(1,128)}, u32[]{:S(2)}) copy-start(s32[1,1,16]{2,1,0:T(1,128)} %param.11) | copy-start | bytes 196
  36.6 33.0 %reduce-scatter.7.cloned.1.call-start = ((), (), s32[]{:S(2)}) async-start(), calls=%async_computation.5 | async-start | bytes 163840 | tf_op jit(solution)/shard_map/reduce_scatter | solution.py:57
  47.2 123.8 %reduce-scatter.9.cloned.1.call-start = ((), (), s32[]{:S(2)}) async-start(), calls=%async_computation.6 | async-start | bytes 98304 | tf_op jit(solution)/shard_map/reduce_scatter | solution.py:54
  163.5 29.1 %reduce-scatter.11.cloned.1.call-start = ((), (), s32[]{:S(2)}) async-start(), calls=%async_computation.7 | async-start | bytes 163840 | tf_op jit(solution)/shard_map/reduce_scatter | solution.py:57
Sparse Core Ops, SparseCore 0:
  36.7 11.1 reduce-scatter.4
  50.1 19.4 reduce-scatter.6
  163.6 7.3 reduce-scatter.8
  173.1 19.4 reduce-scatter.10
where the time goes:
time: 255 us; the launch traced here: 254 us
  blocking collectives  124 us (49%)
  waiting for transfers between devices  45 us (18%)
  other arithmetic  39.1 us (15%)
  matrix products  26.4 us (10%)
  between operations  14.8 us (6%)
  local copies, waits for them, and re-layouts  5.25 us (2%)
    reduce_scatter x2, waiting for transfers between devices, per_device(): lax.psum_scatter(col_terms.reshape(own_width, col_span * BLK), 'row', sca...  43.4 us
    psum x1, blocking collectives, per_device(): lax.psum(jnp.dot(residual_all, residual_all.T, precision=highest), ('row'...  35.3 us
    psum x1, blocking collectives, per_device(): lax.psum((jnp.dot(direction_all, mapped_all.T, precision=highest), jnp.do...  34.3 us
    all_gather x2, blocking collectives, per_device(): lax.all_gather(own_direction, 'row', axis=1, tiled=True)  27.3 us
    another operation x6, other arithmetic, per_device(): jnp.linalg.cholesky(curvature)  13 us
    dot_general x2, matrix products, per_device(): jnp.einsum('csk,smk->csm', col_part[:, cols_here], tile_blocks, precision...  11.4 us
    another operation x4, other arithmetic, per_device(): jax.scipy.linalg.cho_solve((jnp.linalg.cholesky(curvature), True), current)  11.1 us
    all_gather x2, blocking collectives, per_device(): mapped_all = lax.all_gather(mapped, 'depth', axis=0, tiled=True)  10.8 us
  transfers between devices with their start and end apart: 4, of which 4 were waited for; matrix products, arithmetic and copies ran while one was open for 5% of the time, Pallas kernels for 0%

commit v1 on v0

--- a/solution.py
+++ b/solution.py
@@ -30,7 +30,7 @@
         row_part = lax.all_gather(own_direction, "col", axis=1, tiled=True).reshape(
             own_width, row_span, BLK
         )
-        col_part = lax.all_gather(own_direction, "row", axis=1, tiled=True).reshape(
+        col_part = jnp.concatenate(lax.all_gather(own_direction, "row"), axis=1).reshape(
             own_width, col_span, BLK
         )
         live_mask = (slot_index < live_count).astype(jnp.float32)

time: 255 us -> 255 us (level)
  no operation moved by 1% of the time
where the time goes in v1:
time: 255 us
  blocking collectives  124 us (49%)
  waiting for transfers between devices  45 us (18%)
  other arithmetic  39.1 us (15%)
  matrix products  26.4 us (10%)
  between operations  14.8 us (6%)
  local copies, waits for them, and re-layouts  5.6 us (2%)
    reduce_scatter x2, waiting for transfers between devices, per_device(): lax.psum_scatter(col_terms.reshape(own_width, col_span * BLK), 'row', sca...  43.3 us
    psum x1, blocking collectives, per_device(): lax.psum(jnp.dot(residual_all, residual_all.T, precision=highest), ('row'...  35.3 us
    psum x1, blocking collectives, per_device(): lax.psum((jnp.dot(direction_all, mapped_all.T, precision=highest), jnp.do...  34.5 us
    all_gather x2, blocking collectives, per_device(): lax.all_gather(own_direction, 'row')  27.3 us
    another operation x6, other arithmetic, per_device(): jnp.linalg.cholesky(curvature)  13 us
    dot_general x2, matrix products, per_device(): jnp.einsum('csk,smk->csm', col_part[:, cols_here], tile_blocks, precision...  11.4 us
    another operation x4, other arithmetic, per_device(): jax.scipy.linalg.cho_solve((jnp.linalg.cholesky(curvature), True), current)  11.1 us
    all_gather x2, blocking collectives, per_device(): mapped_all = lax.all_gather(mapped, 'depth', axis=0, tiled=True)  10.8 us
  transfers between devices with their start and end apart: 4, of which 4 were waited for; matrix products, arithmetic and copies ran while one was open for 5% of the time, Pallas kernels for 0%

profile of v1, /device:TPU:0, one launch (start us, length us, event | category | flops | bytes accessed | tf_op | source)
XLA Modules:
  0.0 254.8 jit_solution(4442863936200090541)
XLA Ops:
  7.2 6.7 %all_gather.27 = f32[64,512]{1,0:T(8,128)S(1)} all-gather(f32[16,512]{1,0:T(8,128)} %param.8), channel_id=1, replica_groups=mesh['row'=4,'col'=2,'depth'=4] {'depth'}, dimensions={0}, use_global_device_ids=true | all-gather | bytes 163840 | tf_op jit(solution)/shard_map/all_gather | solution.py:22
  13.9 13.9 %all-gather = f32[64,512]{1,0:T(8,128)S(1)} all-gather(f32[16,512]{1,0:T(8,128)S(1)} %constant_dynamic-slice_fusion.1), channel_id=2, replica_groups=mesh['row'=4,'col'=2,'depth'=4] {'row'}, dimensions={0}, use_global_device_ids=true | all-gather | bytes 163840 | tf_op jit(solution)/shard_map/all_gather | solution.py:33
  27.9 0.1 copy.61
  28.1 0.7 fusion.57
  29.4 0.6 gather_fusion
  30.0 5.7 %fusion.6 = f32[16,16,256]{2,1,0:T(8,128)S(1)} fusion(f32[1,1,16,256,256]{4,3,2,1,0:T(8,128)} %param.9, f32[16,16,256]{2,1,0:T(8,128)S(1)} %gather_fusion), kind=kOutput, calls=%fused_computation.10 | convolution fusion | flops 201326592 | bytes 4718592 | tf_op jit(solution)/shard_map/csk,smk->csm/dot_general | solution.py:38
  35.7 0.4 fusion.17
  36.1 0.6 copy.36
  36.8 4.6 %all_gather.30 = f32[16,1024]{1,0:T(8,128)S(1)} all-gather(f32[16,512]{1,0:T(8,128)S(1)} %constant_dynamic-slice_fusion.1), channel_id=1, replica_groups=mesh['row'=4,'col'=2,'depth'=4] {'col'}, dimensions={1}, use_global_device_ids=true | all-gather | bytes 98304 | tf_op jit(solution)/shard_map/all_gather | solution.py:30
  41.4 0.6 gather_fusion.1
  42.0 4.3 %fusion.4 = f32[16,16,256]{2,1,0:T(8,128)S(1)} fusion(f32[1,1,16,256,256]{4,3,2,1,0:T(8,128)} %param.9, f32[16,16,256]{2,1,0:T(8,128)S(1)} %gather_fusion.1), kind=kOutput, calls=%fused_computation.8 | convolution fusion | flops 201326592 | bytes 4718592 | tf_op jit(solution)/shard_map/csm,smk->csk/dot_general | solution.py:41
  46.3 0.4 fusion.14
  46.7 0.7 copy.37
  47.4 0.3 fusion.59
  47.7 0.3 reduce-scatter.5.cloned.1.call-done
  48.0 21.8 %reduce-scatter.7.cloned.1.call-done = f32[16,512]{1,0:T(8,128)} async-done(((f32[16,2048]{1,0:T(8,128)}), f32[16,512]{1,0:T(8,128)}) %reduce-scatter.7.cloned.1.call-update) | async-done | bytes 32784 | tf_op jit(solution)/shard_map/reduce_scatter | solution.py:57
  69.8 0.8 add.75
  70.6 5.4 %all_gather.31 = f32[64,512]{1,0:T(8,128)S(1)} all-gather(f32[16,512]{1,0:T(8,128)S(1)} %add.75), channel_id=1, replica_groups=mesh['row'=4,'col'=2,'depth'=4] {'depth'}, dimensions={0}, use_global_device_ids=true | all-gather | bytes 163840 | tf_op jit(solution)/shard_map/all_gather | solution.py:61
  76.0 0.3 convolution_bitcast_fusion
  76.2 0.3 fusion.61
  76.5 35.3 %all-reduce = (f32[64,64]{0,1:T(8,128)S(1)}, f32[64,64]{0,1:T(8,128)S(1)}, f32[64,64]{1,0:T(8,128)S(1)}) all-reduce(f32[64,64]{0,1:T(8,128)S(1)} %fusion.59, f32[64,64]{0,1:T(8,128)S(1)} %convolution_bitcast_fusion, f32[64,64]{1,0:T(8,128)S(1)} %fusion.61), channel_id=1, replica_groups=mesh['row'=4,'col'=2,'depth'=4] {'row','col'}, use_global_device_ids=true, to_apply=%region_5.7 | all-reduce | flops 12288 | bytes 98304 | tf_op jit(solution)/shard_map/psum | solution.py:25
  112.0 5.8 %cholesky.59 = f32[64,64]{1,0:T(8,128)S(1)} custom-call(f32[64,64]{1,0:T(8,128)S(1)} %get-tuple-element.8), custom_call_target="Cholesky" | custom-call | tf_op jit(solution)/shard_map/jit(cholesky)/cholesky | solution.py:70
  117.9 0.6 compare_reduce_fusion.2
  118.5 0.7 fusion.24
  119.2 4.9 %custom-call.9 = f32[1,64,64]{1,2,0:T(8,128)S(1)} custom-call(f32[1,64,64]{2,1,0:T(8,128)S(1)} %fusion.24), custom_call_target="InvertDiagBlocksLowerTriangular" | custom-call | tf_op jit(solution)/shard_map/jit(_cho_solve)/triangular_solve | solution.py:70
  124.1 0.2 fusion.39
  124.4 0.2 fusion.37
  124.6 0.3 convolution_subtract_fusion
  124.9 0.2 fusion.60
  125.1 0.2 fusion.62
  125.4 5.9 %cholesky.70 = f32[64,64]{1,0:T(8,128)S(1)} custom-call(f32[64,64]{1,0:T(8,128)S(1)} %get-tuple-element.7), custom_call_target="Cholesky" | custom-call | tf_op jit(solution)/shard_map/jit(cholesky)/cholesky | solution.py:87
  131.3 0.6 compare_reduce_fusion.1
  131.9 0.7 fusion.25
  132.6 4.9 %custom-call.10 = f32[1,64,64]{1,2,0:T(8,128)S(1)} custom-call(f32[1,64,64]{2,1,0:T(8,128)S(1)} %fusion.25), custom_call_target="InvertDiagBlocksLowerTriangular" | custom-call | tf_op jit(solution)/shard_map/jit(_cho_solve)/triangular_solve | solution.py:87
  137.5 0.3 convolution_add_fusion.2
  137.7 0.2 fusion.34
  138.0 0.2 fusion.32
  138.1 0.3 convolution_add_fusion
  138.5 13.3 %all-gather.1 = f32[64,512]{1,0:T(8,128)S(1)} all-gather(f32[16,512]{1,0:T(8,128)S(1)} %constant_dynamic-slice_fusion), channel_id=3, replica_groups=mesh['row'=4,'col'=2,'depth'=4] {'row'}, dimensions={0}, use_global_device_ids=true | all-gather | bytes 163840 | tf_op jit(solution)/shard_map/all_gather | solution.py:33
  151.8 4.6 %all_gather.34 = f32[16,1024]{1,0:T(8,128)S(1)} all-gather(f32[16,512]{1,0:T(8,128)S(1)} %constant_dynamic-slice_fusion), channel_id=1, replica_groups=mesh['row'=4,'col'=2,'depth'=4] {'col'}, dimensions={1}, use_global_device_ids=true | all-gather | bytes 98304 | tf_op jit(solution)/shard_map/all_gather | solution.py:30
  156.6 0.6 gather_fusion.2
  157.2 5.7 %fusion.2 = f32[16,16,256]{2,1,0:T(8,128)S(1)} fusion(f32[1,1,16,256,256]{4,3,2,1,0:T(8,128)} %param.9, f32[16,16,256]{2,1,0:T(8,128)S(1)} %gather_fusion.2), kind=kOutput, calls=%fused_computation.6 | convolution fusion | flops 201326592 | bytes 4718592 | tf_op jit(solution)/shard_map/csk,smk->csm/dot_general | solution.py:38
  162.9 0.4 fusion.11
  163.3 0.6 copy.38
  164.0 0.6 gather_fusion.3
  164.5 4.3 %fusion = f32[16,16,256]{2,1,0:T(8,128)S(1)} fusion(f32[1,1,16,256,256]{4,3,2,1,0:T(8,128)} %param.9, f32[16,16,256]{2,1,0:T(8,128)S(1)} %gather_fusion.3), kind=kOutput, calls=%fused_computation.4 | convolution fusion | flops 201326592 | bytes 4718592 | tf_op jit(solution)/shard_map/csm,smk->csk/dot_general | solution.py:41
  168.9 0.4 fusion.8
  169.2 0.7 copy.39
  169.9 0.2 fusion.43
  170.1 1.3 reduce-scatter.9.cloned.1.call-done
  171.4 21.6 %reduce-scatter.11.cloned.1.call-done = f32[16,512]{1,0:T(8,128)} async-done(((f32[16,2048]{1,0:T(8,128)}), f32[16,512]{1,0:T(8,128)}) %reduce-scatter.11.cloned.1.call-update) | async-done | bytes 32784 | tf_op jit(solution)/shard_map/reduce_scatter | solution.py:57
  193.0 0.8 add.78
  193.7 5.4 %all_gather.35 = f32[64,512]{1,0:T(8,128)S(1)} all-gather(f32[16,512]{1,0:T(8,128)S(1)} %add.78), channel_id=1, replica_groups=mesh['row'=4,'col'=2,'depth'=4] {'depth'}, dimensions={0}, use_global_device_ids=true | all-gather | bytes 163840 | tf_op jit(solution)/shard_map/all_gather | solution.py:61
  199.1 0.3 fusion.63
  199.4 34.5 %psum.34 = f32[64,64]{0,1:T(8,128)S(1)} all-reduce(f32[64,64]{0,1:T(8,128)S(1)} %fusion.63), channel_id=1, replica_groups=mesh['row'=4,'col'=2,'depth'=4] {'row','col'}, use_global_device_ids=true, to_apply=%region_9.12 | all-reduce | flops 4096 | bytes 32768 | tf_op jit(solution)/shard_map/psum | solution.py:62
  234.0 5.8 %cholesky.81 = f32[64,64]{1,0:T(8,128)S(1)} custom-call(f32[64,64]{1,0:T(8,128)S(1)} %fusion.31), custom_call_target="Cholesky" | custom-call | tf_op jit(solution)/shard_map/jit(cholesky)/cholesky | solution.py:70
  239.9 0.6 compare_reduce_fusion
  240.6 0.7 fusion.26
  241.2 4.9 %custom-call.11 = f32[1,64,64]{1,2,0:T(8,128)S(1)} custom-call(f32[1,64,64]{2,1,0:T(8,128)S(1)} %fusion.26), custom_call_target="InvertDiagBlocksLowerTriangular" | custom-call | tf_op jit(solution)/shard_map/jit(_cho_solve)/triangular_solve | solution.py:70
  246.1 0.2 fusion.29
  246.4 0.2 fusion.27
  246.6 0.3 fusion.64
  246.9 0.8 convolution_add_fusion.1
  247.7 0.6 dynamic-slice_subtract_fusion
  (35 shorter events, 1.0 us)
Async XLA Ops:
  7.2 28.6 %copy-start = (s32[1,1,16]{2,1,0:T(1,128)S(1)}, s32[1,1,16]{2,1,0:T(1,128)}, u32[]{:S(2)}) copy-start(s32[1,1,16]{2,1,0:T(1,128)} %param.10) | copy-start | bytes 196
  7.2 40.9 %reduce-scatter.5.cloned.1.call-start = ((), (), s32[]{:S(2)}) async-start(), calls=%async_computation.4 | async-start | bytes 98304 | tf_op jit(solution)/shard_map/reduce_scatter | solution.py:54
  30.0 16.3 %copy-start.1 = (s32[1,1,16]{2,1,0:T(1,128)S(1)}, s32[1,1,16]{2,1,0:T(1,128)}, u32[]{:S(2)}) copy-start(s32[1,1,16]{2,1,0:T(1,128)} %param.11) | copy-start | bytes 196
  36.7 33.0 %reduce-scatter.7.cloned.1.call-start = ((), (), s32[]{:S(2)}) async-start(), calls=%async_computation.5 | async-start | bytes 163840 | tf_op jit(solution)/shard_map/reduce_scatter | solution.py:57
  47.4 124.0 %reduce-scatter.9.cloned.1.call-start = ((), (), s32[]{:S(2)}) async-start(), calls=%async_computation.6 | async-start | bytes 98304 | tf_op jit(solution)/shard_map/reduce_scatter | solution.py:54
  163.9 29.0 %reduce-scatter.11.cloned.1.call-start = ((), (), s32[]{:S(2)}) async-start(), calls=%async_computation.7 | async-start | bytes 163840 | tf_op jit(solution)/shard_map/reduce_scatter | solution.py:57
Sparse Core Ops, SparseCore 0:
  36.9 11.1 reduce-scatter.4
  50.3 19.4 reduce-scatter.6
  164.0 7.3 reduce-scatter.8
  173.5 19.4 reduce-scatter.10
